TPU v7x, 32 devices: a whole 2x2x4 slice. The times are simulated.
32 devices in a mesh: dp: 4 (over z), vocab: 8 (over y, x, core).
Axes of the slice: x: 2, y: 2, z: 4, core: 2. Of those that a mesh axis runs over, the one named last changes fastest.
Arguments:
- packed_symbol_codes: int32 [32, 1024], P(('dp', 'vocab')), may hold values from 0 to 50256
- article_numbering: int32 [32, 1024], P(('dp', 'vocab')), may hold values from 0 to 19, never falling along the last dimension, each value on 1 to 256 neighbouring positions
- target_spots: int32 [32, 128], P(('dp', 'vocab')), may hold values from 0 to 1022
- answer_flags: int32 [32, 128], P(('dp', 'vocab')), may hold values 0 or 1
- shared_embedding: bfloat16 [50304, 1024], P('vocab'), may hold values from -0.6 to 0.6
- spot_embedding: bfloat16 [1024, 1024], replicated, may hold values from -0.359375 to 0.359375
- combined_qkv_weights: bfloat16 [1024, 3072], replicated, may hold values from -0.1875 to 0.1875
- attend_outgoing_weights: bfloat16 [1024, 1024], replicated, may hold values from -0.5 to 0.5
- dense_incoming_weights: bfloat16 [1024, 4096], replicated, may hold values from -0.1875 to 0.1875
- dense_outgoing_weights: bfloat16 [4096, 1024], replicated, may hold values from -0.09375 to 0.09375
- layernorm_affine: float32 [6, 1024], replicated, may hold values from -0.6 to 1.3, as said below
- bias_terms: float32 [9216], replicated, may hold values from -1.2 to 1.2
- adaptor_float_copies: float32 [73728], replicated, may hold values from -0.09375 to 0.09375
- average_moments: float32 [73728], replicated, may hold values from -1.2276159e-07 to 1.2276159e-07
- squared_moments: float32 [73728], replicated, may hold values from 1.3576945e-16 to 5.430778e-16
Outputs:
- refreshed_thin_pairs: float32 [73728], replicated
- updated_first_moment: float32 [73728], replicated
- updated_second_moment: float32 [73728], replicated
- gradient_global_norm: float32 [], replicated
- smoothed_entropy_cost: float32 [], replicated
Inputs may be any that keep to these rules, and one draw needn't show every extreme that they name: `article_numbering`: within a slot the document numbers never fall, every document has 1 to 256 tokens. `layernorm_affine`: rows 0 to 2 are gains, rows 3 to 5 shifts.
All inputs are finite; a program needn't handle non-finite values. No bound on the sum of `answer_flags` on one device may be relied on, other than what follows from the above.
Results may differ from a plain program's by a relative error of at most 0.00085.
The roundings to bfloat16 on the way count: a program that leaves them out, or rounds other values in their place, can miss the bound.
Values may be sent and summed in bfloat16 or wider, within the bound.
A program may use at most 320 MiB of HBM per device.

v0:
```python
from functools import partial
import math
import jax
import jax.numpy as jnp
from jax import lax
from jax.sharding import PartitionSpec as P

MODEL_WIDTH = 1024
HEADS = 16
FEEDFWD_UNITS = 4096
VOCAB_SIZE = 50257
RANK = 4
STEP = 10
ADAPTER_SCALE = 8.0
NORM_EPS = 1e-05
GRAD_CLIP = 0.0001
STRIDE_LENGTH = 0.02
BETA_ONE = 0.9
BETA_TWO = 0.999
SHRINK_PENALTY = 0.01
STABILITY_FLOOR = 1e-08
MASKED = -1e30


def matrix_multiply(left, right):
    return jnp.dot(left, right, preferred_element_type=jnp.float32)


def matrix_multiply_transposed_left(left, right):
    return lax.dot_general(
        left, right, (((0,), (0,)), ((), ())), preferred_element_type=jnp.float32
    )


def matrix_multiply_transposed_right(left, right):
    return lax.dot_general(
        left, right, (((1,), (1,)), ((), ())), preferred_element_type=jnp.float32
    )


def layer_norm(stream, gain, shift):
    centred = stream - jnp.mean(stream, axis=-1, keepdims=True)
    spread = lax.rsqrt(jnp.mean(centred * centred, axis=-1, keepdims=True) + NORM_EPS)
    return centred * spread * gain + shift


def positions(segments):
    steps_here = jnp.arange(segments.shape[0], dtype=jnp.int32)
    earlier = (segments[None, :] == segments[:, None]) & (steps_here[None, :] < steps_here[:, None])
    return jnp.sum(earlier.astype(jnp.int32), axis=1)


def distinct_thin_pairs(stacked_samples):
    shapes = [
        (MODEL_WIDTH, 3 * RANK),
        (3, RANK, MODEL_WIDTH),
        (MODEL_WIDTH, RANK),
        (RANK, MODEL_WIDTH),
        (MODEL_WIDTH, RANK),
        (RANK, FEEDFWD_UNITS),
        (FEEDFWD_UNITS, RANK),
        (RANK, MODEL_WIDTH),
    ]
    pieces = []
    offset = 0
    for shape in shapes:
        number = math.prod(shape)
        pieces.append(stacked_samples[offset : offset + number].reshape(shape))
        offset += number
    return pieces


def block_diagonal_mask(blocks):
    number, rank, width = blocks.shape
    eye = jnp.eye(number, dtype=blocks.dtype)
    return (eye[:, None, :, None] * blocks[:, :, None, :]).reshape(number * rank, number * width)


def select_rows(onehot, rows):
    return matrix_multiply(onehot, rows).astype(jnp.bfloat16)


def split_heads(rows):
    return rows.reshape(rows.shape[0], HEADS, rows.shape[1] // HEADS)


def logit_grads(masked_logits, log_total, hit, active_positions, row_weight, denom):
    grad_logits = (row_weight / denom)[:, None] * (
        jnp.exp(masked_logits - log_total[:, None])
        - 0.9 * hit.astype(jnp.float32)
        - 0.1 / VOCAB_SIZE * active_positions.astype(jnp.float32)[None, :]
    )
    return grad_logits.astype(jnp.bfloat16)


def adaptive_moment_update(grad, weight, first, second):
    first_new = BETA_ONE * first + (1.0 - BETA_ONE) * grad
    second_new = BETA_TWO * second + (1.0 - BETA_TWO) * grad * grad
    debiased_mean_estimate = first_new / (1.0 - BETA_ONE**STEP)
    debiased_variance_estimate = second_new / (1.0 - BETA_TWO**STEP)
    weight_new = weight - STRIDE_LENGTH * (
        debiased_mean_estimate / (jnp.sqrt(debiased_variance_estimate) + STABILITY_FLOOR)
        + SHRINK_PENALTY * weight
    )
    return (weight_new, first_new, second_new)


def local(
    packed_symbol_codes,
    article_numbering,
    target_spots,
    answer_flags,
    shared_embedding,
    spot_embedding,
    combined_qkv_weights,
    attend_outgoing_weights,
    dense_incoming_weights,
    dense_outgoing_weights,
    layernorm_affine,
    bias_terms,
    adaptor_float_copies,
    average_moments,
    squared_moments,
):
    tokens_here = packed_symbol_codes[0]
    segments = article_numbering[0]
    spot_objective = target_spots[0]
    rows_here = spot_objective.shape[0]
    shard_rows = shared_embedding.shape[0]
    table_base = lax.axis_index("vocab") * shard_rows
    all_tokens = lax.all_gather(packed_symbol_codes, "vocab", axis=0, tiled=True).reshape(-1)
    wanted = all_tokens - table_base
    inside = (wanted >= 0) & (wanted < shard_rows)
    picked = jnp.take(shared_embedding, jnp.clip(wanted, 0, shard_rows - 1), axis=0)
    embedded = lax.psum_scatter(
        jnp.where(inside[:, None], picked.astype(jnp.float32), 0.0).astype(jnp.bfloat16),
        "vocab",
        scatter_dimension=0,
        tiled=True,
    ).astype(jnp.float32)
    stream = embedded + jnp.take(spot_embedding, positions(segments), axis=0).astype(jnp.float32)
    a_qkv, b_qkv, a_o, b_o, a_fc, b_fc, a_p, b_p = [
        lexicon_portion.astype(jnp.bfloat16)
        for lexicon_portion in distinct_thin_pairs(adaptor_float_copies)
    ]
    width = stream.shape[1]
    hidden_width = dense_incoming_weights.shape[1]
    length = stream.shape[0]
    onehot = spot_objective[:, None] == jnp.arange(length, dtype=jnp.int32)[None, :]
    pick = onehot.astype(jnp.bfloat16)
    h1 = layer_norm(stream, layernorm_affine[0], layernorm_affine[3]).astype(jnp.bfloat16)
    stream_rows = jnp.take(stream, spot_objective, axis=0)
    h1_rows = select_rows(pick, h1)
    u1 = matrix_multiply(h1, a_qkv).astype(jnp.bfloat16)
    u1_rows = select_rows(pick, u1)
    q = (
        matrix_multiply(h1_rows, combined_qkv_weights[:, :width])
        + bias_terms[:width]
        + ADAPTER_SCALE * matrix_multiply(u1_rows[:, :RANK], b_qkv[0])
    ).astype(jnp.bfloat16)
    kv = (
        matrix_multiply(h1, combined_qkv_weights[:, width:])
        + bias_terms[width : 3 * width]
        + ADAPTER_SCALE * matrix_multiply(u1[:, RANK:], block_diagonal_mask(b_qkv[1:]))
    ).astype(jnp.bfloat16)
    queries, keys_all, values_all = (
        split_heads(q),
        split_heads(kv[:, :width]),
        split_heads(kv[:, width:]),
    )
    scale = queries.shape[2] ** (-0.5)
    there = jnp.arange(length, dtype=jnp.int32)[None, :]
    segment_rows = jnp.take(segments, spot_objective)
    allowed = (there <= spot_objective[:, None]) & (segment_rows[:, None] == segments[None, :])
    scores = (
        jnp.einsum("qhd,khd->hqk", queries, keys_all, preferred_element_type=jnp.float32) * scale
    )
    scores = jnp.where(allowed[None], scores, MASKED)
    top = jnp.max(scores, axis=2, keepdims=True)
    expd = jnp.exp(scores - top)
    probs = expd / jnp.sum(expd, axis=2, keepdims=True)
    probs_low = probs.astype(jnp.bfloat16)
    o = (
        jnp.einsum("hqk,khd->qhd", probs_low, values_all, preferred_element_type=jnp.float32)
        .reshape(rows_here, width)
        .astype(jnp.bfloat16)
    )
    uo = matrix_multiply(o, a_o).astype(jnp.bfloat16)
    middle = (
        stream_rows
        + matrix_multiply(o, attend_outgoing_weights)
        + bias_terms[3 * width : 4 * width]
        + ADAPTER_SCALE * matrix_multiply(uo, b_o)
    )
    h2, norm_two_back = jax.vjp(
        lambda value: layer_norm(value, layernorm_affine[1], layernorm_affine[4]), middle
    )
    h2 = h2.astype(jnp.bfloat16)
    uf = matrix_multiply(h2, a_fc).astype(jnp.bfloat16)
    pre = (
        matrix_multiply(h2, dense_incoming_weights)
        + bias_terms[4 * width : 4 * width + hidden_width]
        + ADAPTER_SCALE * matrix_multiply(uf, b_fc)
    )
    f, gelu_back = jax.vjp(partial(jax.nn.gelu, approximate=True), pre)
    f = f.astype(jnp.bfloat16)
    up = matrix_multiply(f, a_p).astype(jnp.bfloat16)
    output = (
        middle
        + matrix_multiply(f, dense_outgoing_weights)
        + bias_terms[4 * width + hidden_width :]
        + ADAPTER_SCALE * matrix_multiply(up, b_p)
    )
    closing_result, final_back = jax.vjp(
        lambda value: layer_norm(value, layernorm_affine[2], layernorm_affine[5]), output
    )
    final_rows = closing_result.astype(jnp.bfloat16)
    next_places = spot_objective + 1
    targets = jnp.take(tokens_here, next_places)
    weights_here = answer_flags[0] * (
        jnp.take(segments, spot_objective) == jnp.take(segments, next_places)
    ).astype(jnp.int32)
    all_labels = lax.all_gather(
        jnp.stack([targets, weights_here], axis=1), "vocab", axis=0, tiled=True
    )
    class_scores = matrix_multiply_transposed_right(
        lax.all_gather(final_rows, "vocab", axis=0, tiled=True), shared_embedding
    )
    vocab_ids = table_base + jnp.arange(shard_rows, dtype=jnp.int32)
    active_positions = vocab_ids < VOCAB_SIZE
    masked_logits = jnp.where(active_positions[None, :], class_scores, -jnp.inf)
    local_top = jnp.max(masked_logits, axis=1)
    smooth_local = jnp.sum(jnp.where(active_positions[None, :], class_scores, 0.0), axis=1)
    hit = vocab_ids[None, :] == all_labels[:, 0:1]
    target_local = jnp.sum(jnp.where(hit, class_scores, 0.0), axis=1)
    top = lax.pmax(local_top, "vocab")
    local_sum = jnp.sum(jnp.exp(masked_logits - top[:, None]), axis=1)
    exp_sum, smooth_sum, target_logit = lax.psum((local_sum, smooth_local, target_local), "vocab")
    log_total = top + jnp.log(exp_sum)
    row_weight = all_labels[:, 1].astype(jnp.float32)
    row_loss = log_total - 0.9 * target_logit - 0.1 * smooth_sum / VOCAB_SIZE
    loss_sum, weight_sum = lax.psum((jnp.sum(row_weight * row_loss), jnp.sum(row_weight)), "dp")
    denom = jnp.maximum(weight_sum, 1.0)
    smoothed_entropy_cost = loss_sum / denom
    grad_logits = logit_grads(masked_logits, log_total, hit, active_positions, row_weight, denom)
    grad_rows = lax.psum_scatter(
        matrix_multiply(
            lax.slice_in_dim(grad_logits, 0, rows_here * lax.axis_size("vocab"), axis=0),
            shared_embedding,
        ),
        "vocab",
        scatter_dimension=0,
        tiled=True,
    )
    same = spot_objective[:, None] == spot_objective[None, :]
    order = jnp.arange(rows_here, dtype=jnp.int32)
    repeat = jnp.any(same & (order[None, :] < order[:, None]), axis=1)
    merge = (same & ~repeat[:, None]).astype(jnp.float32)
    grad_final = jnp.dot(merge, grad_rows, precision=lax.Precision.HIGHEST)
    (dx3,) = final_back(grad_final)
    dm = dx3.astype(jnp.bfloat16)
    g_bp = ADAPTER_SCALE * matrix_multiply_transposed_left(up, dm)
    du_p = (ADAPTER_SCALE * matrix_multiply_transposed_right(dm, b_p)).astype(jnp.bfloat16)
    g_ap = matrix_multiply_transposed_left(f, du_p)
    df = matrix_multiply_transposed_right(
        dm, dense_outgoing_weights
    ) + matrix_multiply_transposed_right(du_p, a_p)
    (dpre,) = gelu_back(df)
    dpre = dpre.astype(jnp.bfloat16)
    g_bfc = ADAPTER_SCALE * matrix_multiply_transposed_left(uf, dpre)
    du_f = (ADAPTER_SCALE * matrix_multiply_transposed_right(dpre, b_fc)).astype(jnp.bfloat16)
    g_afc = matrix_multiply_transposed_left(h2, du_f)
    dh2 = matrix_multiply_transposed_right(
        dpre, dense_incoming_weights
    ) + matrix_multiply_transposed_right(du_f, a_fc)
    (grad_middle,) = norm_two_back(dh2)
    dx2 = dx3 + grad_middle
    da = dx2.astype(jnp.bfloat16)
    g_bo = ADAPTER_SCALE * matrix_multiply_transposed_left(uo, da)
    du_o = (ADAPTER_SCALE * matrix_multiply_transposed_right(da, b_o)).astype(jnp.bfloat16)
    g_ao = matrix_multiply_transposed_left(o, du_o)
    do = (
        matrix_multiply_transposed_right(da, attend_outgoing_weights)
        + matrix_multiply_transposed_right(du_o, a_o)
    ).astype(jnp.bfloat16)
    do = split_heads(do)
    dv = jnp.einsum("hqk,qhd->khd", probs_low, do, preferred_element_type=jnp.float32)
    dp = jnp.einsum("qhd,khd->hqk", do, values_all, preferred_element_type=jnp.float32)
    ds = (probs * (dp - jnp.sum(probs * dp, axis=2, keepdims=True))).astype(jnp.bfloat16)
    dq = jnp.einsum("hqk,khd->qhd", ds, keys_all, preferred_element_type=jnp.float32) * scale
    dk = jnp.einsum("hqk,qhd->khd", ds, queries, preferred_element_type=jnp.float32) * scale
    dq = dq.reshape(rows_here, width).astype(jnp.bfloat16)
    dk = dk.reshape(length, width).astype(jnp.bfloat16)
    dv = dv.reshape(length, width).astype(jnp.bfloat16)
    thirds = ((h1_rows, u1_rows, dq), (h1, u1, dk), (h1, u1, dv))
    g_bqkv = []
    g_aqkv = []
    for j, (normed, low, grad) in enumerate(thirds):
        low = low[:, j * RANK : (j + 1) * RANK]
        g_bqkv.append(ADAPTER_SCALE * matrix_multiply_transposed_left(low, grad))
        du = (ADAPTER_SCALE * matrix_multiply_transposed_right(grad, b_qkv[j])).astype(jnp.bfloat16)
        g_aqkv.append(matrix_multiply_transposed_left(normed, du))
    pieces = [
        jnp.concatenate(g_aqkv, axis=1),
        jnp.concatenate(g_bqkv, axis=0),
        g_ao,
        g_bo,
        g_afc,
        g_bfc,
        g_ap,
        g_bp,
    ]
    local_grad = jnp.concatenate([piece.reshape(-1) for piece in pieces])
    grad_total = lax.psum(local_grad, ("dp", "vocab"))
    gradient_global_norm = jnp.sqrt(jnp.sum(grad_total * grad_total))
    capped_derivative = grad_total * (GRAD_CLIP / jnp.maximum(gradient_global_norm, GRAD_CLIP))
    refreshed_thin_pairs, updated_first_moment, updated_second_moment = adaptive_moment_update(
        capped_derivative, adaptor_float_copies, average_moments, squared_moments
    )
    return (
        refreshed_thin_pairs,
        updated_first_moment,
        updated_second_moment,
        gradient_global_norm,
        smoothed_entropy_cost,
    )


def solution(mesh):
    return jax.shard_map(
        local,
        mesh=mesh,
        in_specs=(
            P(("dp", "vocab"), None),
            P(("dp", "vocab"), None),
            P(("dp", "vocab"), None),
            P(("dp", "vocab"), None),
            P("vocab", None),
            P(),
            P(),
            P(),
            P(),
            P(),
            P(),
            P(),
            P(),
            P(),
            P(),
        ),
        out_specs=(P(), P(), P(), P(), P()),
        check_vma=False,
    )
```

profile of v0, /device:TPU:8, one launch (start us, length us, event | category | flops | bytes accessed | tf_op | source)
XLA Modules:
  0.0 644.7 jit_solution(2936452298662439854)
XLA Ops:
  7.2 9.4 %all-gather = s32[8,1,1024]{2,1,0:T(1,128)S(1)} all-gather(s32[1,1,1024]{2,1,0:T(1,128)} %bitcast.159), channel_id=1, replica_groups=mesh['dp'=4,'vocab'=8] {'vocab'}, dimensions={0}, use_global_device_ids=true | all-gather | bytes 36864 | tf_op jit(solution)/shard_map/all_gather | solution.py:131
  16.9 47.0 %gather_fusion = bf16[8192,1024]{1,0:T(8,128)(2,1)} fusion(bf16[6288,1024]{1,0:T(8,128)(2,1)} %param.21, s32[8192]{0:T(1024)S(1)} %broadcast_clamp_fusion), kind=kCustom, calls=%fused_computation.3 | custom fusion | bytes 33587200 | tf_op jit(solution)/shard_map/jit(_take)/gather | solution.py:134
  63.9 15.2 %select_convert_fusion = bf16[8192,1024]{1,0:T(8,128)(2,1)} fusion(bf16[8192,1024]{1,0:T(8,128)(2,1)} %gather_fusion, pred[8192]{0:T(1024)(128)(4,1)S(1)} %compare_and_fusion.3, pred[8192]{0:T(1024)(128)(4,1)S(1)} %bitcast.197), kind=kLoop, calls=%fused_computation.7 | loop fusion | flops 33554432 | bytes 33570816 | tf_op jit(solution)/shard_map/convert_element_type | solution.py:136
  90.2 5.4 gather_fusion.1
  98.8 96.5 %reduce-scatter.3.cloned.1.call-done = bf16[1024,1024]{1,0:T(8,128)(2,1)} async-done(((bf16[8192,1024]{1,0:T(8,128)(2,1)}), bf16[1024,1024]{1,0:T(8,128)(2,1)}) %reduce-scatter.3.cloned.1.call-update) | async-done | bytes 2097168 | tf_op jit(solution)/shard_map/reduce_scatter | solution.py:135
  195.4 3.2 fusion.92
  203.9 6.8 %fusion.12 = f32[1024,2048]{1,0:T(8,128)} fusion(bf16[1024,1024]{1,0:T(8,128)(2,1)S(1)} %add_convert_fusion.1, bf16[1024,3072]{1,0:T(8,128)(2,1)S(1)} %bitcast.214), kind=kOutput, calls=%fused_computation.34 | convolution fusion | flops 4294967296 | bytes 14680064 | tf_op jit(solution)/shard_map/dot_general | solution.py:26
  211.6 4.8 add_convert_fusion
  216.4 2.5 fusion.93
  218.9 2.9 copy.44
  221.8 4.8 copy.46
  226.5 4.2 gather_fusion.2
  230.7 6.3 fusion.98
  237.6 6.1 fusion.44
  247.0 2.4 multiply_convert_fusion.2
  252.9 8.8 %all_gather.10 = s32[1024,2]{0,1:T(2,128)S(1)} all-gather(s32[128,2]{0,1:T(2,128)S(1)} %pad_add_fusion), channel_id=1, replica_groups=mesh['dp'=4,'vocab'=8] {'vocab'}, dimensions={0}, use_global_device_ids=true | all-gather | bytes 9216 | tf_op jit(solution)/shard_map/all_gather | solution.py:223
  263.0 17.9 %all-gather.3.cloned.1.call-done = bf16[1024,1024]{1,0:T(8,128)(2,1)} async-done(((bf16[128,1024]{1,0:T(8,128)(2,1)}), bf16[1024,1024]{1,0:T(8,128)(2,1)}) %all-gather.3.cloned.1.call-update) | async-done | bytes 2097168 | tf_op jit(solution)/shard_map/all_gather | solution.py:227
  280.8 23.6 %select_reduce_fusion.1 = (f32[1024]{0:T(1024)S(1)}, f32[1024,6288]{0,1:T(8,128)}) fusion(pred[6288]{0:T(1024)(128)(4,1)S(1)} %broadcast_compare_fusion, bf16[1024,1024]{1,0:T(8,128)(2,1)} %all-gather.3.cloned.1.call-done, bf16[6288,1024]{1,0:T(8,128)(2,1)} %param.21), kind=kOutput, calls=%fused_computation.17 | convolution fusion | flops 13199768576 | bytes 40741008 | tf_op jit(solution)/shard_map/dot_general | solution.py:36
  304.5 13.1 %pmax.7 = f32[1024]{0:T(1024)S(1)} all-reduce(f32[1024]{0:T(1024)S(1)} %get-tuple-element.61), channel_id=1, replica_groups=mesh['dp'=4,'vocab'=8] {'vocab'}, use_global_device_ids=true, to_apply=%region_14.16 | all-reduce | flops 1024 | bytes 8192 | tf_op jit(solution)/shard_map/pmax | solution.py:236
  317.6 12.1 %select_reduce_fusion = (f32[1024]{0:T(1024)S(1)}, f32[1024]{0:T(1024)S(1)}, f32[1024]{0:T(1024)S(1)}) fusion(f32[1024,6288]{0,1:T(8,128)} %get-tuple-element.62, pred[6288]{0:T(1024)(128)(4,1)S(1)} %broadcast_compare_fusion, f32[1024]{0:T(1024)S(1)} %pmax.7, s32[1024]{0:T(1024)S(1)} %bitcast.202, s32[6288]{0:T(1024)S(1)} %iota_add_fusion), kind=kLoop, calls=%fused_computation.15 | loop fusion | flops 51508224 | bytes 25807568 | tf_op jit(solution)/shard_map/reduce_sum | solution.py:233
  329.7 22.3 %all-reduce = (f32[1024]{0:T(1024)}, f32[1024]{0:T(1024)}, f32[1024]{0:T(1024)}) all-reduce(f32[1024]{0:T(1024)S(1)} %get-tuple-element.7, f32[1024]{0:T(1024)S(1)} %get-tuple-element.6, f32[1024]{0:T(1024)S(1)} %get-tuple-element.8), channel_id=1, replica_groups=mesh['dp'=4,'vocab'=8] {'vocab'}, use_global_device_ids=true, to_apply=%region_16.18 | all-reduce | flops 3072 | bytes 24576 | tf_op jit(solution)/shard_map/psum | solution.py:238
  353.3 9.5 %all-reduce.1 = (f32[]{:T(128)}, f32[]{:T(128)}) all-reduce(f32[]{:T(128)} %fusion.88, f32[]{:T(128)} %get-tuple-element.21), channel_id=1, replica_groups=mesh['dp'=4,'vocab'=8] {'dp'}, use_global_device_ids=true, to_apply=%region_8.10 | all-reduce | flops 2 | bytes 16 | tf_op jit(solution)/shard_map/psum | solution.py:242
  363.5 28.8 %fusion.6 = f32[1024,1024]{1,0:T(8,128)} fusion(bf16[6288,1024]{1,0:T(8,128)(2,1)} %param.21, f32[1024,6288]{0,1:T(8,128)} %get-tuple-element.62, f32[6288]{0:T(1024)} %broadcast_select_fusion, s32[1024]{0:T(1024)S(1)} %bitcast.203, f32[1024]{0:T(1024)S(1)} %get-tuple-element.22, f32[1024]{0:T(1024)S(1)} %bitcast.212, s32[6288]{0:T(1024)S(1)} %iota_add_fusion, ...), kind=kOutput, calls=%fused_computation.18 | convolution fusion | flops 13238403072 | bytes 42896656 | tf_op jit(solution)/shard_map/dot_general | solution.py:26
  394.4 50.1 %reduce-scatter.5.cloned.1.call-done = f32[128,1024]{1,0:T(8,128)} async-done(((f32[1024,1024]{1,0:T(8,128)}), f32[128,1024]{1,0:T(8,128)}) %reduce-scatter.5.cloned.1.call-update) | async-done | bytes 524304 | tf_op jit(solution)/shard_map/reduce_scatter | solution.py:246
  447.4 6.4 fusion.101
  458.1 2.9 fusion.102
  464.6 5.9 multiply_reduce_fusion
  479.5 3.9 reshape.410
  486.4 2.2 convolution_multiply_fusion.9
  488.7 3.1 fusion.53
  491.8 3.0 fusion.52
  504.3 127.0 %all-reduce.4.cloned.1.call-done = f32[73728]{0:T(1024)} async-done(((f32[73728]{0:T(1024)}), f32[73728]{0:T(1024)}) %all-reduce.4.cloned.1.call-update) | async-done | bytes 294928 | tf_op jit(solution)/shard_map/psum | solution.py:314
  (301 shorter events, 67.3 us)
Async XLA Ops:
  7.2 83.0 %copy-start = (bf16[1024,1024]{1,0:T(8,128)(2,1)S(1)}, bf16[1024,1024]{1,0:T(8,128)(2,1)}, u32[]{:S(2)}) copy-start(bf16[1024,1024]{1,0:T(8,128)(2,1)} %param.22) | copy-start | bytes 6291460
  7.2 188.2 %reduce-scatter.3.cloned.1.call-start = ((), (), s32[]{:S(2)}) async-start(), calls=%async_computation.2 | async-start | bytes 18874368 | tf_op jit(solution)/shard_map/reduce_scatter | solution.py:135
  79.2 201.7 %all-gather.3.cloned.1.call-start = ((), (), s32[]{:S(2)}) async-start(), calls=%async_computation.3 | async-start | bytes 2359296 | tf_op jit(solution)/shard_map/all_gather | solution.py:227
  81.4 129.7 %copy-start.31 = (bf16[4,1024]{1,0:T(4,128)(2,1)}, bf16[4,1024]{1,0:T(4,128)(2,1)S(1)}, u32[]{:S(2)}) copy-start(bf16[4,1024]{1,0:T(4,128)(2,1)S(1)} %squeeze.21) | copy-start | bytes 24580
  90.2 6.6 %copy-start.34 = (f32[9216]{0:T(1024)S(1)}, f32[9216]{0:T(1024)}, u32[]{:S(2)}) copy-start(f32[9216]{0:T(1024)} %param.28) | copy-start | bytes 110596
  90.2 7.2 %copy-start.37 = (f32[6,1024]{1,0:T(8,128)S(1)}, f32[6,1024]{1,0:T(8,128)}, u32[]{:S(2)}) copy-start(f32[6,1024]{1,0:T(8,128)} %param.27) | copy-start | bytes 73732
  200.7 10.0 %copy-start.5 = (bf16[1024,1024]{1,0:T(8,128)(2,1)}, bf16[1024,1024]{1,0:T(8,128)(2,1)S(1)}, u32[]{:S(2)}) copy-start(bf16[1024,1024]{1,0:T(8,128)(2,1)S(1)} %add_convert_fusion.1) | copy-start | bytes 6291460
  202.7 8.0 %copy-start.20 = (bf16[128,1024]{1,0:T(8,128)(2,1)}, bf16[128,1024]{1,0:T(8,128)(2,1)S(1)}, u32[]{:S(2)}) copy-start(bf16[128,1024]{1,0:T(8,128)(2,1)S(1)} %convolution_convert_fusion) | copy-start | bytes 786436
  203.3 8.3 %copy-start.29 = (bf16[1024,12]{0,1:T(8,128)(2,1)}, bf16[1024,12]{0,1:T(8,128)(2,1)S(1)}, u32[]{:S(2)}) copy-start(bf16[1024,12]{0,1:T(8,128)(2,1)S(1)} %convolution_convert_fusion.1) | copy-start | bytes 73732
  203.9 7.3 %copy-start.53 = (bf16[128,12]{0,1:T(8,128)(2,1)}, bf16[128,12]{0,1:T(8,128)(2,1)S(1)}, u32[]{:S(2)}) copy-start(bf16[128,12]{0,1:T(8,128)(2,1)S(1)} %fusion.61) | copy-start | bytes 9220
  211.6 19.1 %copy-start.21 = (bf16[128,1024]{0,1:T(8,128)(2,1)}, bf16[128,1024]{0,1:T(8,128)(2,1)S(1)}, u32[]{:S(2)}) copy-start(bf16[128,1024]{0,1:T(8,128)(2,1)S(1)} %copy.45) | copy-start | bytes 786436
  221.8 8.9 %copy-start.7 = (bf16[1024,1024]{0,1:T(8,128)(2,1)}, bf16[1024,1024]{0,1:T(8,128)(2,1)S(1)}, u32[]{:S(2)}) copy-start(bf16[1024,1024]{0,1:T(8,128)(2,1)S(1)} %copy.44) | copy-start | bytes 6291460
  237.0 8.5 %slice-start.2 = ((s8[8388608]{0:T(1024)(128)(4,1)}), s8[4194304]{0:T(1024)(128)(4,1)S(1)}, s32[]{:S(2)}) async-start(s8[8388608]{0:T(1024)(128)(4,1)} %bitcast.163), calls=%async_computation.8 | async-start | bytes 8388608
  237.6 7.9 %slice-start.3 = ((s8[8388608]{0:T(1024)(128)(4,1)}), s8[4194304]{0:T(1024)(128)(4,1)S(1)}, s32[]{:S(2)}) async-start(s8[8388608]{0:T(1024)(128)(4,1)} %bitcast.163), calls=%async_computation.9 | async-start | bytes 8388608
  251.7 52.8 %copy-start.51 = (f32[128]{0:T(128)}, f32[128]{0:T(128)S(1)}, u32[]{:S(2)}) copy-start(f32[128]{0:T(128)S(1)} %broadcast_multiply_fusion.2) | copy-start | bytes 1540
  251.9 9.8 %copy-start.67 = (f32[128]{0:T(128)}, f32[128]{0:T(128)S(1)}, u32[]{:S(2)}) copy-start(f32[128]{0:T(128)S(1)} %multiply_reduce_fusion.4) | copy-start | bytes 1540
  251.9 9.8 %copy-start.59 = (f32[128]{0:T(128)}, f32[128]{0:T(128)S(1)}, u32[]{:S(2)}) copy-start(f32[128]{0:T(128)S(1)} %fusion.80) | copy-start | bytes 1540
  252.8 191.7 %reduce-scatter.5.cloned.1.call-start = ((), (), s32[]{:S(2)}) async-start(), calls=%async_computation.4 | async-start | bytes 4718592 | tf_op jit(solution)/shard_map/reduce_scatter | solution.py:246
  392.3 52.2 %copy-start.52 = (f32[128]{0:T(128)S(1)}, f32[128]{0:T(128)}, u32[]{:S(2)}) copy-start(f32[128]{0:T(128)} %copy-done.51) | copy-start | bytes 1540
  392.3 53.8 %copy-start.68 = (f32[128]{0:T(128)S(1)}, f32[128]{0:T(128)}, u32[]{:S(2)}) copy-start(f32[128]{0:T(128)} %copy-done.67) | copy-start | bytes 1540
  392.3 53.8 %copy-start.60 = (f32[128]{0:T(128)S(1)}, f32[128]{0:T(128)}, u32[]{:S(2)}) copy-start(f32[128]{0:T(128)} %copy-done.59) | copy-start | bytes 1540
  392.4 238.9 %all-reduce.4.cloned.1.call-start = ((), (), s32[]{:S(2)}) async-start(), calls=%async_computation.5 | async-start | bytes 589824 | tf_op jit(solution)/shard_map/psum | solution.py:314
  447.4 8.2 %copy-start.69 = (f32[128,4096]{1,0:T(8,128)S(1)}, f32[128,4096]{1,0:T(8,128)}, u32[]{:S(2)}) copy-start(f32[128,4096]{1,0:T(8,128)} %get-tuple-element.58) | copy-start | bytes 6291460
  447.4 10.5 %slice-start.4 = ((s8[8388608]{0:T(1024)(128)(4,1)}), s8[4194304]{0:T(1024)(128)(4,1)S(1)}, s32[]{:S(2)}) async-start(s8[8388608]{0:T(1024)(128)(4,1)} %bitcast.165), calls=%async_computation.10 | async-start | bytes 8388608
  464.6 6.5 %slice-start.7 = ((s8[8388608]{0:T(1024)(128)(4,1)}), s8[4194304]{0:T(1024)(128)(4,1)S(1)}, s32[]{:S(2)}) async-start(s8[8388608]{0:T(1024)(128)(4,1)} %bitcast.171), calls=%async_computation.13 | async-start | bytes 8388608
  475.3 10.4 %copy-start.6 = (bf16[16,64,1024]{2,1,0:T(8,128)(2,1)}, bf16[16,64,1024]{2,1,0:T(8,128)(2,1)S(1)}, u32[]{:S(2)}) copy-start(bf16[16,64,1024]{2,1,0:T(8,128)(2,1)S(1)} %multiply_convert_fusion.1) | copy-start | bytes 6291460
  477.5 8.3 %copy-start.30 = (bf16[1024,12]{0,1:T(8,128)(2,1)S(1)}, bf16[1024,12]{0,1:T(8,128)(2,1)}, u32[]{:S(2)}) copy-start(bf16[1024,12]{0,1:T(8,128)(2,1)} %copy-done.29) | copy-start | bytes 73732
  479.5 9.2 %copy-start.36 = (bf16[4,1024]{1,0:T(4,128)(2,1)S(1)}, bf16[4,1024]{1,0:T(4,128)(2,1)}, u32[]{:S(2)}) copy-start(bf16[4,1024]{1,0:T(4,128)(2,1)} %squeeze.25) | copy-start | bytes 24580
  488.7 147.0 %copy-start.1 = (bf16[1024,1024]{1,0:T(8,128)(2,1)S(1)}, bf16[1024,1024]{1,0:T(8,128)(2,1)}, u32[]{:S(2)}) copy-start(bf16[1024,1024]{1,0:T(8,128)(2,1)} %param.22) | copy-start | bytes 6291460
  491.8 141.9 %copy-start.19 = (f32[73728]{0:T(1024)S(1)}, f32[73728]{0:T(1024)}, u32[]{:S(2)}) copy-start(f32[73728]{0:T(1024)} %param.29) | copy-start | bytes 884740
  491.8 141.9 %copy-start.25 = (f32[73728]{0:T(1024)S(1)}, f32[73728]{0:T(1024)}, u32[]{:S(2)}) copy-start(f32[73728]{0:T(1024)} %param.30) | copy-start | bytes 884740
  491.8 141.9 %copy-start.26 = (f32[73728]{0:T(1024)S(1)}, f32[73728]{0:T(1024)}, u32[]{:S(2)}) copy-start(f32[73728]{0:T(1024)} %param.31) | copy-start | bytes 884740
  (54 other events, 171.8 us)
Sparse Core Ops, SparseCore 0:
  79.3 116.0 reduce-scatter.2
  252.9 27.8 all-gather.2
  392.5 51.9 reduce-scatter.4
  503.7 127.4 all-reduce.3
where the time goes:
time: 650 us; the launch traced here: 645 us
  waiting for transfers between devices  292 us (45%)
  matrix products  126 us (19%)
  local copies, waits for them, and re-layouts  98.7 us (15%)
  blocking collectives  63 us (10%)
  other arithmetic  45.7 us (7%)
  between operations  19.6 us (3%)
    psum x1, waiting for transfers between devices, local(): grad_total = lax.psum(local_grad, ('dp', 'vocab'))  127 us
    reduce_scatter x1, waiting for transfers between devices, local(): lax.psum_scatter(jnp.where(inside[:, None], picked.astype(jnp.float32), 0...  96.5 us
    reduce_scatter x1, waiting for transfers between devices, local(): lax.psum_scatter(matrix_multiply(lax.slice_in_dim(grad_logits, 0, rows_he...  50.1 us
    dot_general x17, matrix products, matrix_multiply(): return jnp.dot(left, right, preferred_element_type=jnp.float32)  49.7 us
    gather x1, local copies, waits for them, and re-layouts, local(): jnp.take(shared_embedding, jnp.clip(wanted, 0, shard_rows - 1), axis=0)  47 us
    dot_general x10, matrix products, matrix_multiply_transposed_right(): lax.dot_general(left, right, (((1,), (1,)), ((), ())), preferred_element_...  36.9 us
    psum x1, blocking collectives, local(): lax.psum((local_sum, smooth_local, target_local), 'vocab')  22.3 us
    all_gather x1, waiting for transfers between devices, local(): lax.all_gather(final_rows, 'vocab', axis=0, tiled=True)  17.9 us
  transfers between devices with their start and end apart: 4, of which 4 were waited for; matrix products, arithmetic and copies ran while one was open for 3% of the time, Pallas kernels for 0%

commit v1 on v0

--- a/solution.py
+++ b/solution.py
@@ -311,7 +311,7 @@
         g_bp,
     ]
     local_grad = jnp.concatenate([piece.reshape(-1) for piece in pieces])
-    grad_total = lax.psum(local_grad, ("dp", "vocab"))
+    grad_total = lax.psum(lax.psum(local_grad, "vocab"), "dp")
     gradient_global_norm = jnp.sqrt(jnp.sum(grad_total * grad_total))
     capped_derivative = grad_total * (GRAD_CLIP / jnp.maximum(gradient_global_norm, GRAD_CLIP))
     refreshed_thin_pairs, updated_first_moment, updated_second_moment = adaptive_moment_update(

time: 650 us -> 615 us (0.946)
  waiting for transfers between devices: 292 us -> 255 us
    psum x1 -> x2, waiting for transfers between devices: 127 us -> 90.7 us  [local(): grad_total = lax.psum(lax.psum(local_grad, 'vocab'), 'dp')]
  transfers between devices with their start and end apart: 4 -> 5, of which waited for: 4 -> 5; matrix products, arithmetic and copies ran while one was open for 3% -> 3% of each run, Pallas kernels for 0% -> 0%
where the time goes in v1:
time: 615 us; the launch traced here: 609 us
  waiting for transfers between devices  255 us (41%)
  matrix products  126 us (20%)
  local copies, waits for them, and re-layouts  98.7 us (16%)
  blocking collectives  63 us (10%)
  other arithmetic  45.7 us (7%)
  between operations  19.6 us (3%)
    reduce_scatter x1, waiting for transfers between devices, local(): lax.psum_scatter(jnp.where(inside[:, None], picked.astype(jnp.float32), 0...  96.5 us
    psum x2, waiting for transfers between devices, local(): grad_total = lax.psum(lax.psum(local_grad, 'vocab'), 'dp')  90.7 us
    reduce_scatter x1, waiting for transfers between devices, local(): lax.psum_scatter(matrix_multiply(lax.slice_in_dim(grad_logits, 0, rows_he...  50.1 us
    dot_general x17, matrix products, matrix_multiply(): return jnp.dot(left, right, preferred_element_type=jnp.float32)  49.7 us
    gather x1, local copies, waits for them, and re-layouts, local(): jnp.take(shared_embedding, jnp.clip(wanted, 0, shard_rows - 1), axis=0)  47 us
    dot_general x10, matrix products, matrix_multiply_transposed_right(): lax.dot_general(left, right, (((1,), (1,)), ((), ())), preferred_element_...  36.9 us
    psum x1, blocking collectives, local(): lax.psum((local_sum, smooth_local, target_local), 'vocab')  22.3 us
    all_gather x1, waiting for transfers between devices, local(): lax.all_gather(final_rows, 'vocab', axis=0, tiled=True)  17.9 us
  transfers between devices with their start and end apart: 5, of which 5 were waited for; matrix products, arithmetic and copies ran while one was open for 3% of the time, Pallas kernels for 0%

profile of v1, /device:TPU:8, one launch (start us, length us, event | category | flops | bytes accessed | tf_op | source)
XLA Modules:
  0.0 608.5 jit_solution(8338679920212168969)
XLA Ops:
  7.2 9.4 %all-gather = s32[8,1,1024]{2,1,0:T(1,128)S(1)} all-gather(s32[1,1,1024]{2,1,0:T(1,128)} %bitcast.159), channel_id=1, replica_groups=mesh['dp'=4,'vocab'=8] {'vocab'}, dimensions={0}, use_global_device_ids=true | all-gather | bytes 36864 | tf_op jit(solution)/shard_map/all_gather | solution.py:131
  16.9 47.0 %gather_fusion = bf16[8192,1024]{1,0:T(8,128)(2,1)} fusion(bf16[6288,1024]{1,0:T(8,128)(2,1)} %param.21, s32[8192]{0:T(1024)S(1)} %broadcast_clamp_fusion), kind=kCustom, calls=%fused_computation.3 | custom fusion | bytes 33587200 | tf_op jit(solution)/shard_map/jit(_take)/gather | solution.py:134
  63.9 15.2 %select_convert_fusion = bf16[8192,1024]{1,0:T(8,128)(2,1)} fusion(bf16[8192,1024]{1,0:T(8,128)(2,1)} %gather_fusion, pred[8192]{0:T(1024)(128)(4,1)S(1)} %compare_and_fusion.3, pred[8192]{0:T(1024)(128)(4,1)S(1)} %bitcast.197), kind=kLoop, calls=%fused_computation.7 | loop fusion | flops 33554432 | bytes 33570816 | tf_op jit(solution)/shard_map/convert_element_type | solution.py:136
  90.2 5.4 gather_fusion.1
  98.8 96.5 %reduce-scatter.3.cloned.1.call-done = bf16[1024,1024]{1,0:T(8,128)(2,1)} async-done(((bf16[8192,1024]{1,0:T(8,128)(2,1)}), bf16[1024,1024]{1,0:T(8,128)(2,1)}) %reduce-scatter.3.cloned.1.call-update) | async-done | bytes 2097168 | tf_op jit(solution)/shard_map/reduce_scatter | solution.py:135
  195.4 3.2 fusion.92
  203.9 6.8 %fusion.12 = f32[1024,2048]{1,0:T(8,128)} fusion(bf16[1024,1024]{1,0:T(8,128)(2,1)S(1)} %add_convert_fusion.1, bf16[1024,3072]{1,0:T(8,128)(2,1)S(1)} %bitcast.214), kind=kOutput, calls=%fused_computation.34 | convolution fusion | flops 4294967296 | bytes 14680064 | tf_op jit(solution)/shard_map/dot_general | solution.py:26
  211.6 4.8 add_convert_fusion
  216.4 2.5 fusion.93
  218.9 2.9 copy.44
  221.8 4.8 copy.46
  226.5 4.2 gather_fusion.2
  230.7 6.3 %fusion.98 = (f32[16,128]{1,0:T(8,128)S(1)}, f32[16,128,1024]{2,1,0:T(8,128)}) fusion(pred[128,1024]{1,0:T(8,128)(4,1)} %fusion.62, bf16[128,16,64]{0,2,1:T(8,128)(2,1)S(1)} %bitcast.182, bf16[1024,16,64]{0,2,1:T(8,128)(2,1)S(1)} %bitcast.169), kind=kOutput, calls=%fused_computation.217 | convolution fusion | flops 276825088 | bytes 10887168 | tf_op jit(solution)/shard_map/sub | solution.py:180
  237.6 6.1 fusion.44
  247.0 2.4 multiply_convert_fusion.2
  252.9 8.8 %all_gather.10 = s32[1024,2]{0,1:T(2,128)S(1)} all-gather(s32[128,2]{0,1:T(2,128)S(1)} %pad_add_fusion), channel_id=1, replica_groups=mesh['dp'=4,'vocab'=8] {'vocab'}, dimensions={0}, use_global_device_ids=true | all-gather | bytes 9216 | tf_op jit(solution)/shard_map/all_gather | solution.py:223
  263.0 17.9 %all-gather.3.cloned.1.call-done = bf16[1024,1024]{1,0:T(8,128)(2,1)} async-done(((bf16[128,1024]{1,0:T(8,128)(2,1)}), bf16[1024,1024]{1,0:T(8,128)(2,1)}) %all-gather.3.cloned.1.call-update) | async-done | bytes 2097168 | tf_op jit(solution)/shard_map/all_gather | solution.py:227
  280.8 23.6 %select_reduce_fusion.1 = (f32[1024]{0:T(1024)S(1)}, f32[1024,6288]{0,1:T(8,128)}) fusion(pred[6288]{0:T(1024)(128)(4,1)S(1)} %broadcast_compare_fusion, bf16[1024,1024]{1,0:T(8,128)(2,1)} %all-gather.3.cloned.1.call-done, bf16[6288,1024]{1,0:T(8,128)(2,1)} %param.21), kind=kOutput, calls=%fused_computation.17 | convolution fusion | flops 13199768576 | bytes 40741008 | tf_op jit(solution)/shard_map/dot_general | solution.py:36
  304.5 13.1 %pmax.7 = f32[1024]{0:T(1024)S(1)} all-reduce(f32[1024]{0:T(1024)S(1)} %get-tuple-element.61), channel_id=1, replica_groups=mesh['dp'=4,'vocab'=8] {'vocab'}, use_global_device_ids=true, to_apply=%region_14.16 | all-reduce | flops 1024 | bytes 8192 | tf_op jit(solution)/shard_map/pmax | solution.py:236
  317.6 12.1 %select_reduce_fusion = (f32[1024]{0:T(1024)S(1)}, f32[1024]{0:T(1024)S(1)}, f32[1024]{0:T(1024)S(1)}) fusion(f32[1024,6288]{0,1:T(8,128)} %get-tuple-element.62, pred[6288]{0:T(1024)(128)(4,1)S(1)} %broadcast_compare_fusion, f32[1024]{0:T(1024)S(1)} %pmax.7, s32[1024]{0:T(1024)S(1)} %bitcast.202, s32[6288]{0:T(1024)S(1)} %iota_add_fusion), kind=kLoop, calls=%fused_computation.15 | loop fusion | flops 51508224 | bytes 25807568 | tf_op jit(solution)/shard_map/reduce_sum | solution.py:233
  329.7 22.3 %all-reduce = (f32[1024]{0:T(1024)}, f32[1024]{0:T(1024)}, f32[1024]{0:T(1024)}) all-reduce(f32[1024]{0:T(1024)S(1)} %get-tuple-element.7, f32[1024]{0:T(1024)S(1)} %get-tuple-element.6, f32[1024]{0:T(1024)S(1)} %get-tuple-element.8), channel_id=1, replica_groups=mesh['dp'=4,'vocab'=8] {'vocab'}, use_global_device_ids=true, to_apply=%region_16.18 | all-reduce | flops 3072 | bytes 24576 | tf_op jit(solution)/shard_map/psum | solution.py:238
  353.3 9.5 %all-reduce.1 = (f32[]{:T(128)}, f32[]{:T(128)}) all-reduce(f32[]{:T(128)} %fusion.88, f32[]{:T(128)} %get-tuple-element.21), channel_id=1, replica_groups=mesh['dp'=4,'vocab'=8] {'dp'}, use_global_device_ids=true, to_apply=%region_8.10 | all-reduce | flops 2 | bytes 16 | tf_op jit(solution)/shard_map/psum | solution.py:242
  363.5 28.8 %fusion.6 = f32[1024,1024]{1,0:T(8,128)} fusion(bf16[6288,1024]{1,0:T(8,128)(2,1)} %param.21, f32[1024,6288]{0,1:T(8,128)} %get-tuple-element.62, f32[6288]{0:T(1024)} %broadcast_select_fusion, s32[1024]{0:T(1024)S(1)} %bitcast.203, f32[1024]{0:T(1024)S(1)} %get-tuple-element.22, f32[1024]{0:T(1024)S(1)} %bitcast.212, s32[6288]{0:T(1024)S(1)} %iota_add_fusion, ...), kind=kOutput, calls=%fused_computation.18 | convolution fusion | flops 13238403072 | bytes 42896656 | tf_op jit(solution)/shard_map/dot_general | solution.py:26
  394.4 50.1 %reduce-scatter.5.cloned.1.call-done = f32[128,1024]{1,0:T(8,128)} async-done(((f32[1024,1024]{1,0:T(8,128)}), f32[128,1024]{1,0:T(8,128)}) %reduce-scatter.5.cloned.1.call-update) | async-done | bytes 524304 | tf_op jit(solution)/shard_map/reduce_scatter | solution.py:246
  447.4 6.4 %fusion.101 = f32[128,4096]{1,0:T(8,128)S(1)} fusion(bf16[128,1024]{1,0:T(8,128)(2,1)S(1)} %add_convert_fusion.5, bf16[4096,1024]{1,0:T(8,128)(2,1)} %param.26), kind=kOutput, calls=%fused_computation.220 | convolution fusion | flops 1073741824 | bytes 10747904 | tf_op jit(solution)/shard_map/dot_general | solution.py:36
  458.1 2.9 fusion.102
  464.6 5.9 multiply_reduce_fusion
  479.5 3.9 reshape.410
  488.7 3.1 fusion.53
  491.8 3.0 fusion.52
  503.7 53.2 %all-reduce.5.cloned.1.call-done = f32[73728]{0:T(1024)} async-done(((f32[73728]{0:T(1024)}), f32[73728]{0:T(1024)}) %all-reduce.5.cloned.1.call-update) | async-done | bytes 294928 | tf_op jit(solution)/shard_map/psum | solution.py:314
  557.5 37.6 %all-reduce.7.cloned.1.call-done = f32[73728]{0:T(1024)} async-done(((f32[73728]{0:T(1024)}), f32[73728]{0:T(1024)}) %all-reduce.7.cloned.1.call-update) | async-done | bytes 294928 | tf_op jit(solution)/shard_map/psum | solution.py:314
  (304 shorter events, 69.6 us)
Async XLA Ops:
  7.2 83.0 %copy-start = (bf16[1024,1024]{1,0:T(8,128)(2,1)S(1)}, bf16[1024,1024]{1,0:T(8,128)(2,1)}, u32[]{:S(2)}) copy-start(bf16[1024,1024]{1,0:T(8,128)(2,1)} %param.22) | copy-start | bytes 6291460
  7.2 188.2 %reduce-scatter.3.cloned.1.call-start = ((), (), s32[]{:S(2)}) async-start(), calls=%async_computation.2 | async-start | bytes 18874368 | tf_op jit(solution)/shard_map/reduce_scatter | solution.py:135
  79.2 201.7 %all-gather.3.cloned.1.call-start = ((), (), s32[]{:S(2)}) async-start(), calls=%async_computation.3 | async-start | bytes 2359296 | tf_op jit(solution)/shard_map/all_gather | solution.py:227
  81.4 129.7 %copy-start.31 = (bf16[4,1024]{1,0:T(4,128)(2,1)}, bf16[4,1024]{1,0:T(4,128)(2,1)S(1)}, u32[]{:S(2)}) copy-start(bf16[4,1024]{1,0:T(4,128)(2,1)S(1)} %squeeze.21) | copy-start | bytes 24580
  90.2 6.6 %copy-start.34 = (f32[9216]{0:T(1024)S(1)}, f32[9216]{0:T(1024)}, u32[]{:S(2)}) copy-start(f32[9216]{0:T(1024)} %param.28) | copy-start | bytes 110596
  90.2 7.2 %copy-start.37 = (f32[6,1024]{1,0:T(8,128)S(1)}, f32[6,1024]{1,0:T(8,128)}, u32[]{:S(2)}) copy-start(f32[6,1024]{1,0:T(8,128)} %param.27) | copy-start | bytes 73732
  200.7 10.0 %copy-start.5 = (bf16[1024,1024]{1,0:T(8,128)(2,1)}, bf16[1024,1024]{1,0:T(8,128)(2,1)S(1)}, u32[]{:S(2)}) copy-start(bf16[1024,1024]{1,0:T(8,128)(2,1)S(1)} %add_convert_fusion.1) | copy-start | bytes 6291460
  202.7 8.0 %copy-start.20 = (bf16[128,1024]{1,0:T(8,128)(2,1)}, bf16[128,1024]{1,0:T(8,128)(2,1)S(1)}, u32[]{:S(2)}) copy-start(bf16[128,1024]{1,0:T(8,128)(2,1)S(1)} %convolution_convert_fusion) | copy-start | bytes 786436
  203.3 8.3 %copy-start.29 = (bf16[1024,12]{0,1:T(8,128)(2,1)}, bf16[1024,12]{0,1:T(8,128)(2,1)S(1)}, u32[]{:S(2)}) copy-start(bf16[1024,12]{0,1:T(8,128)(2,1)S(1)} %convolution_convert_fusion.1) | copy-start | bytes 73732
  203.9 7.3 %copy-start.53 = (bf16[128,12]{0,1:T(8,128)(2,1)}, bf16[128,12]{0,1:T(8,128)(2,1)S(1)}, u32[]{:S(2)}) copy-start(bf16[128,12]{0,1:T(8,128)(2,1)S(1)} %fusion.61) | copy-start | bytes 9220
  211.6 19.1 %copy-start.21 = (bf16[128,1024]{0,1:T(8,128)(2,1)}, bf16[128,1024]{0,1:T(8,128)(2,1)S(1)}, u32[]{:S(2)}) copy-start(bf16[128,1024]{0,1:T(8,128)(2,1)S(1)} %copy.45) | copy-start | bytes 786436
  221.8 8.9 %copy-start.7 = (bf16[1024,1024]{0,1:T(8,128)(2,1)}, bf16[1024,1024]{0,1:T(8,128)(2,1)S(1)}, u32[]{:S(2)}) copy-start(bf16[1024,1024]{0,1:T(8,128)(2,1)S(1)} %copy.44) | copy-start | bytes 6291460
  237.0 8.5 %slice-start.2 = ((s8[8388608]{0:T(1024)(128)(4,1)}), s8[4194304]{0:T(1024)(128)(4,1)S(1)}, s32[]{:S(2)}) async-start(s8[8388608]{0:T(1024)(128)(4,1)} %bitcast.163), calls=%async_computation.9 | async-start | bytes 8388608
  237.6 7.9 %slice-start.3 = ((s8[8388608]{0:T(1024)(128)(4,1)}), s8[4194304]{0:T(1024)(128)(4,1)S(1)}, s32[]{:S(2)}) async-start(s8[8388608]{0:T(1024)(128)(4,1)} %bitcast.163), calls=%async_computation.10 | async-start | bytes 8388608
  251.7 52.8 %copy-start.51 = (f32[128]{0:T(128)}, f32[128]{0:T(128)S(1)}, u32[]{:S(2)}) copy-start(f32[128]{0:T(128)S(1)} %broadcast_multiply_fusion.2) | copy-start | bytes 1540
  251.9 9.8 %copy-start.67 = (f32[128]{0:T(128)}, f32[128]{0:T(128)S(1)}, u32[]{:S(2)}) copy-start(f32[128]{0:T(128)S(1)} %multiply_reduce_fusion.4) | copy-start | bytes 1540
  251.9 9.8 %copy-start.59 = (f32[128]{0:T(128)}, f32[128]{0:T(128)S(1)}, u32[]{:S(2)}) copy-start(f32[128]{0:T(128)S(1)} %fusion.80) | copy-start | bytes 1540
  252.8 191.7 %reduce-scatter.5.cloned.1.call-start = ((), (), s32[]{:S(2)}) async-start(), calls=%async_computation.4 | async-start | bytes 4718592 | tf_op jit(solution)/shard_map/reduce_scatter | solution.py:246
  392.3 52.2 %copy-start.52 = (f32[128]{0:T(128)S(1)}, f32[128]{0:T(128)}, u32[]{:S(2)}) copy-start(f32[128]{0:T(128)} %copy-done.51) | copy-start | bytes 1540
  392.3 53.8 %copy-start.68 = (f32[128]{0:T(128)S(1)}, f32[128]{0:T(128)}, u32[]{:S(2)}) copy-start(f32[128]{0:T(128)} %copy-done.67) | copy-start | bytes 1540
  392.3 53.8 %copy-start.60 = (f32[128]{0:T(128)S(1)}, f32[128]{0:T(128)}, u32[]{:S(2)}) copy-start(f32[128]{0:T(128)} %copy-done.59) | copy-start | bytes 1540
  392.4 164.4 %all-reduce.5.cloned.1.call-start = ((), (), s32[]{:S(2)}) async-start(), calls=%async_computation.5 | async-start | bytes 589824 | tf_op jit(solution)/shard_map/psum | solution.py:314
  447.4 8.2 %copy-start.69 = (f32[128,4096]{1,0:T(8,128)S(1)}, f32[128,4096]{1,0:T(8,128)}, u32[]{:S(2)}) copy-start(f32[128,4096]{1,0:T(8,128)} %get-tuple-element.58) | copy-start | bytes 6291460
  447.4 10.5 %slice-start.4 = ((s8[8388608]{0:T(1024)(128)(4,1)}), s8[4194304]{0:T(1024)(128)(4,1)S(1)}, s32[]{:S(2)}) async-start(s8[8388608]{0:T(1024)(128)(4,1)} %bitcast.165), calls=%async_computation.11 | async-start | bytes 8388608
  475.3 10.4 %copy-start.6 = (bf16[16,64,1024]{2,1,0:T(8,128)(2,1)}, bf16[16,64,1024]{2,1,0:T(8,128)(2,1)S(1)}, u32[]{:S(2)}) copy-start(bf16[16,64,1024]{2,1,0:T(8,128)(2,1)S(1)} %multiply_convert_fusion.1) | copy-start | bytes 6291460
  477.5 8.3 %copy-start.30 = (bf16[1024,12]{0,1:T(8,128)(2,1)S(1)}, bf16[1024,12]{0,1:T(8,128)(2,1)}, u32[]{:S(2)}) copy-start(bf16[1024,12]{0,1:T(8,128)(2,1)} %copy-done.29) | copy-start | bytes 73732
  479.5 9.2 %copy-start.36 = (bf16[4,1024]{1,0:T(4,128)(2,1)S(1)}, bf16[4,1024]{1,0:T(4,128)(2,1)}, u32[]{:S(2)}) copy-start(bf16[4,1024]{1,0:T(4,128)(2,1)} %squeeze.25) | copy-start | bytes 24580
  488.7 110.8 %copy-start.1 = (bf16[1024,1024]{1,0:T(8,128)(2,1)S(1)}, bf16[1024,1024]{1,0:T(8,128)(2,1)}, u32[]{:S(2)}) copy-start(bf16[1024,1024]{1,0:T(8,128)(2,1)} %param.22) | copy-start | bytes 6291460
  491.8 105.7 %copy-start.19 = (f32[73728]{0:T(1024)S(1)}, f32[73728]{0:T(1024)}, u32[]{:S(2)}) copy-start(f32[73728]{0:T(1024)} %param.29) | copy-start | bytes 884740
  491.8 105.7 %copy-start.25 = (f32[73728]{0:T(1024)S(1)}, f32[73728]{0:T(1024)}, u32[]{:S(2)}) copy-start(f32[73728]{0:T(1024)} %param.30) | copy-start | bytes 884740
  491.8 105.7 %copy-start.26 = (f32[73728]{0:T(1024)S(1)}, f32[73728]{0:T(1024)}, u32[]{:S(2)}) copy-start(f32[73728]{0:T(1024)} %param.31) | copy-start | bytes 884740
  503.6 91.5 %all-reduce.7.cloned.1.call-start = ((), (), s32[]{:S(2)}) async-start(), calls=%async_computation.6 | async-start | bytes 589824 | tf_op jit(solution)/shard_map/psum | solution.py:314
  (55 other events, 178.3 us)
Sparse Core Ops, SparseCore 0:
  79.3 116.0 reduce-scatter.2
  252.9 27.8 all-gather.2
  392.5 51.9 reduce-scatter.4
  503.7 53.0 all-reduce.4
  559.1 35.9 all-reduce.6
